TPU v7x, 128 devices: a whole 4x4x4 slice. The times are simulated.
128 devices in a mesh: row: 16 (over z_hi, y, core), col: 8 (over z_lo, x).
Axes of the slice: x: 4, y: 4, z: 4 (z_hi: 2, z_lo: 2; z = z_hi * 2 + z_lo), core: 2. Of those that a mesh axis runs over, the one named last changes fastest.
Arguments:
- multispectral: bfloat16 [2, 32768, 4096], P(None, 'row', 'col'), may hold values from -6 to 6
- hyperspectral: bfloat16 [96, 8192, 1024], P(None, 'row', 'col'), may hold values from -6 to 6
- row_start: float32 [32768, 128], P(('row', 'col')), may hold values from -6 to 6
- col_factor: bfloat16 [4096, 128], P('col', 'row'), may hold values from -0.09375 to 0.09375
- band_factor: float32 [96, 128], replicated, may hold values from -2 to 2
- response: float32 [2, 96], replicated, may hold values from 0.2 to 1
- blur_taps: float32 [9], replicated, may hold values from 0.2 to 1
- offsets: int32 [9], replicated, may hold values from -8 to 8, as said below
Outputs:
- row_factor: float32 [32768, 128], P(('row', 'col'))
- residual: float32 [32768, 128], P(('row', 'col'))
Inputs may be any that keep to these rules, and one draw needn't show every extreme that they name: 9 distinct offsets; -8 and 8 are always among them.
All inputs are finite; a program needn't handle non-finite values.
Results may differ from a plain program's by a relative error of at most 0.0023.
Values may be sent and summed in bfloat16 or wider, within the bound.
A program may use at most 128 MiB of HBM per device.

v0:
```python
import jax
import jax.numpy as jnp
from jax import lax
from jax.sharding import PartitionSpec as P

DEC = 4
W = 8
ITERS = 4


RIDGE_TERM = 0.1
FULL_PRECISION = lax.Precision.HIGHEST


def extended(cells, sides, width):
    for axis, dim in sides:
        count = lax.axis_size(axis)
        head = lax.slice_in_dim(cells, 0, width, axis=dim)
        tail = lax.slice_in_dim(cells, cells.shape[dim] - width, cells.shape[dim], axis=dim)
        cells = jnp.concatenate(
            [
                lax.ppermute(tail, axis, [(i, (i + 1) % count) for i in range(count)]),
                cells,
                lax.ppermute(head, axis, [((i + 1) % count, i) for i in range(count)]),
            ],
            axis=dim,
        )
    return cells


def down_matrix(weights, offsets, rows_out, rows_in):
    outer = lax.broadcasted_iota(jnp.int32, (rows_out, rows_in), 0)
    inner = lax.broadcasted_iota(jnp.int32, (rows_out, rows_in), 1)
    total = jnp.zeros((rows_out, rows_in), jnp.float32)
    for number in range(weights.shape[0]):
        target = DEC * outer + offsets[number] + W
        total = total + jnp.where(inner == target, weights[number], jnp.float32(0.0))
    return total


def up_matrix(weights, offsets, rows_in, low_margin):
    rows_out = (rows_in - 2 * low_margin) * DEC
    outer = lax.broadcasted_iota(jnp.int32, (rows_out, rows_in), 0)
    inner = lax.broadcasted_iota(jnp.int32, (rows_out, rows_in), 1)
    total = jnp.zeros((rows_out, rows_in), jnp.float32)
    for number in range(weights.shape[0]):
        target = outer + DEC * low_margin - offsets[number]
        total = total + jnp.where(DEC * inner == target, weights[number], jnp.float32(0.0))
    return total


def apply_band(matrix, values):
    return jnp.dot(matrix, values.astype(jnp.float32), precision=FULL_PRECISION)


def body(
    multispectral, hyperspectral, row_start, col_factor, band_factor, response, blur_taps, offsets
):
    low_reach = (W + DEC - 1) // DEC
    columns = lax.all_gather(col_factor, "row", axis=1, tiled=True)
    column_wide = extended(columns, (("col", 0),), W)
    column_down = down_matrix(blur_taps, offsets, columns.shape[0] // DEC, column_wide.shape[0])
    coarse_columns = apply_band(column_down, column_wide)
    merged = jnp.dot(response, band_factor, precision=FULL_PRECISION)
    multi_pairs = (merged[:, None, :] * columns.astype(jnp.float32)[None, :, :]).astype(
        jnp.bfloat16
    )
    hyper_pairs = (band_factor[:, None, :] * coarse_columns[None, :, :]).astype(jnp.bfloat16)
    multi_part = jnp.einsum(
        "kij,kjr->ir", multispectral, multi_pairs, preferred_element_type=jnp.float32
    )
    hyper_part = jnp.einsum(
        "kij,kjr->ir", hyperspectral, hyper_pairs, preferred_element_type=jnp.float32
    )
    column_part = jnp.einsum("jr,js->rs", columns, columns, preferred_element_type=jnp.float32)
    coarse_part = jnp.einsum("jr,js->rs", coarse_columns, coarse_columns, precision=FULL_PRECISION)
    column_gram, coarse_gram = lax.psum((column_part, coarse_part), "col")
    band_gram = jnp.dot(band_factor.T, band_factor, precision=FULL_PRECISION)
    merged_gram = jnp.dot(merged.T, merged, precision=FULL_PRECISION)
    hyper_gram = coarse_gram * band_gram
    multi_gram = column_gram * merged_gram
    multi_sums, hyper_sums = lax.psum((multi_part, hyper_part), "col")
    start_rows = lax.all_gather(row_start, "col", axis=0, tiled=True)

    def fine_rim(values, breadth):
        return extended(values, (("row", 0),), breadth)

    def coarse_rim(values):
        return extended(values, (("row", 0),), low_reach)

    def inner_sum(first_field, second_field):
        return lax.psum(jnp.sum(first_field * second_field), "row")

    fine_rows = start_rows.shape[0]
    coarse_rows = fine_rows // DEC
    lifting = up_matrix(blur_taps, offsets, coarse_rows + 2 * low_reach, low_reach)
    lowering = down_matrix(blur_taps, offsets, coarse_rows, fine_rows + 2 * W)

    def operate(values):
        fine_wide = fine_rim(values, W)
        coarse_wide = coarse_rim(apply_band(lowering, fine_wide))
        restored = apply_band(lifting, coarse_wide)
        return (
            jnp.dot(restored, hyper_gram, precision=FULL_PRECISION)
            + jnp.dot(values, multi_gram, precision=FULL_PRECISION)
            + RIDGE_TERM * values
        )

    right_side = apply_band(lifting, coarse_rim(hyper_sums)) + multi_sums
    solution = start_rows
    residual = right_side - operate(solution)
    direction = residual
    norm_now = inner_sum(residual, residual)
    for iteration in range(ITERS):
        mapped = operate(direction)
        step_size = norm_now / inner_sum(direction, mapped)
        solution = solution + step_size * direction
        residual = residual - step_size * mapped
        norm_next = inner_sum(residual, residual)
        direction = residual + norm_next / norm_now * direction
        norm_now = norm_next
    portion = solution.shape[0] // lax.axis_size("col")
    corner = lax.axis_index("col") * portion
    solution = lax.dynamic_slice_in_dim(solution, corner, portion, 0)
    residual = lax.dynamic_slice_in_dim(residual, corner, portion, 0)
    return (solution, residual)


def solution(mesh):
    in_specs = (
        P(None, "row", "col"),
        P(None, "row", "col"),
        P(("row", "col"), None),
        P("col", "row"),
        P(),
        P(),
        P(),
        P(),
    )
    out_specs = (P(("row", "col"), None), P(("row", "col"), None))
    return jax.shard_map(body, mesh=mesh, in_specs=in_specs, out_specs=out_specs, check_vma=False)
```

profile of v0, /device:TPU:0, one launch (start us, length us, event | category | flops | bytes accessed | tf_op | source)
XLA Modules:
  0.0 721.7 jit_solution(4614198952941534308)
XLA Ops:
  7.2 25.9 %all_gather.7 = bf16[512,128]{0,1:T(8,128)(2,1)S(1)} all-gather(bf16[512,8]{0,1:T(8,128)(2,1)} %param.11), channel_id=1, replica_groups=mesh['row'=16,'col'=8] {'row'}, dimensions={1}, use_global_device_ids=true | all-gather | bytes 139264 | tf_op jit(solution)/shard_map/all_gather | solution.py:60
  52.6 6.3 fusion.50
  59.9 8.2 %fusion.14 = f32[512,128]{0,1:T(8,128)} fusion(bf16[96,512,128]{2,1,0:T(8,128)(2,1)} %param.9, f32[128,128]{0,1:T(8,128)S(1)} %copy.10, f32[96,128]{1,0:T(8,128)S(1)} %copy-done.4), kind=kOutput, calls=%fused_computation.33 | convolution fusion | flops 1613758464 | bytes 12959744 | tf_op jit(solution)/shard_map/kij,kjr->ir/dot_general | solution.py:72
  79.9 62.0 %all-reduce.4.cloned.1.call-done = (f32[128,128]{1,0:T(8,128)}, f32[128,128]{1,0:T(8,128)}, f32[2048,128]{1,0:T(8,128)}, f32[512,128]{0,1:T(8,128)}) async-done(((f32[128,128]{1,0:T(8,128)}, f32[128,128]{1,0:T(8,128)}, f32[2048,128]{1,0:T(8,128)}, f32[512,128]{0,1:T(8,128)}), (f32[128,128]{1,0:T(8,128)}, f32[128,128]{1,0:T(8,128)}, f32[2048,128]{1,0:T(8,128)}, ...) | async-done | bytes 1441808 | tf_op jit(solution)/shard_map/psum | solution.py:77
  143.0 39.1 %all-gather.2.cloned.1.call-done = f32[2048,128]{1,0:T(8,128)} async-done(((f32[256,128]{1,0:T(8,128)}), f32[2048,128]{1,0:T(8,128)}) %all-gather.2.cloned.1.call-update) | async-done | bytes 1048592 | tf_op jit(solution)/shard_map/all_gather | solution.py:83
  189.7 15.4 %fusion.13 = f32[512,128]{1,0:T(8,128)S(1)} fusion(f32[]{:T(128)} %bitcast.17, s32[512]{0:T(512)S(1)} %get-tuple-element.63, f32[]{:T(128)} %bitcast.15, s32[512]{0:T(512)S(1)} %get-tuple-element.64, f32[]{:T(128)} %bitcast.13, s32[512]{0:T(512)S(1)} %get-tuple-element.65, f32[]{:T(128)} %bitcast.11, s32[512]{0:T(512)S(1)} %get-tuple-element.66, ...), kind=kOutput, calls=%fused_computation.32 | convolution fusion | flops 1651200000 | bytes 1337380 | tf_op jit(solution)/shard_map/dot_general | solution.py:53
  216.6 14.6 %fusion.19 = f32[2048,128]{1,0:T(8,128)S(1)} fusion(f32[]{:T(128)} %bitcast.17, f32[]{:T(128)} %bitcast.15, f32[]{:T(128)} %bitcast.13, f32[]{:T(128)} %bitcast.11, f32[]{:T(128)} %bitcast.9, f32[]{:T(128)} %bitcast.7, f32[]{:T(128)} %bitcast.5, f32[]{:T(128)} %bitcast.3, f32[]{:T(128)} %bitcast.1, s32[516]{0:T(1024)S(1)} %iota_multiply_fusion, ...), kind=kOutput, calls=%fused_computation.40 | convolution fusion | flops 1650803712 | bytes 1388596 | tf_op jit(solution)/shard_map/dot_general | solution.py:53
  233.4 15.0 %fusion.3 = f32[2048,128]{1,0:T(8,128)S(1)} fusion(f32[2048,128]{1,0:T(8,128)S(1)} %fusion.5, f32[2048,128]{1,0:T(8,128)S(1)} %copy-done.8, f32[]{:T(128)} %bitcast.17, f32[]{:T(128)} %bitcast.15, f32[]{:T(128)} %bitcast.13, f32[]{:T(128)} %bitcast.11, f32[]{:T(128)} %bitcast.9, f32[]{:T(128)} %bitcast.7, f32[]{:T(128)} %bitcast.5, f32[]{:T(128)} %bitcast.3, ...), kind=kOutput, calls=%fused_computation.18 | convolution fusion | flops 1651328000 | bytes 3485748 | tf_op jit(solution)/shard_map/dot_general | solution.py:53
  255.3 14.2 %fusion.12 = f32[512,128]{1,0:T(8,128)S(1)} fusion(f32[]{:T(128)} %bitcast.17, s32[512]{0:T(512)S(1)} %get-tuple-element.63, f32[]{:T(128)} %bitcast.15, s32[512]{0:T(512)S(1)} %get-tuple-element.64, f32[]{:T(128)} %bitcast.13, s32[512]{0:T(512)S(1)} %get-tuple-element.65, f32[]{:T(128)} %bitcast.11, s32[512]{0:T(512)S(1)} %get-tuple-element.66, ...), kind=kOutput, calls=%fused_computation.31 | convolution fusion | flops 1651200000 | bytes 1337380 | tf_op jit(solution)/shard_map/dot_general | solution.py:53
  269.6 5.8 collective-permute-start.11
  276.7 14.7 %fusion.18 = f32[2048,128]{1,0:T(8,128)S(1)} fusion(f32[]{:T(128)} %bitcast.17, f32[]{:T(128)} %bitcast.15, f32[]{:T(128)} %bitcast.13, f32[]{:T(128)} %bitcast.11, f32[]{:T(128)} %bitcast.9, f32[]{:T(128)} %bitcast.7, f32[]{:T(128)} %bitcast.5, f32[]{:T(128)} %bitcast.3, f32[]{:T(128)} %bitcast.1, s32[516]{0:T(1024)S(1)} %iota_multiply_fusion, ...), kind=kOutput, calls=%fused_computation.39 | convolution fusion | flops 1650803712 | bytes 1388596 | tf_op jit(solution)/shard_map/dot_general | solution.py:53
  294.1 39.1 %all-reduce = (f32[]{:T(128)}, f32[]{:T(128)}) all-reduce(f32[]{:T(128)} %get-tuple-element.3, f32[]{:T(128)} %get-tuple-element.2), channel_id=1, replica_groups=mesh['row'=16,'col'=8] {'row'}, use_global_device_ids=true, to_apply=%region_5.6 | all-reduce | flops 2 | bytes 16 | tf_op jit(solution)/shard_map/psum | solution.py:92
  335.4 33.9 %psum.90 = f32[]{:T(128)} all-reduce(f32[]{:T(128)} %multiply_reduce_fusion.5), channel_id=1, replica_groups=mesh['row'=16,'col'=8] {'row'}, use_global_device_ids=true, to_apply=%region_9.10 | all-reduce | flops 1 | bytes 8 | tf_op jit(solution)/shard_map/psum | solution.py:92
  377.7 14.1 %fusion.11 = f32[512,128]{1,0:T(8,128)S(1)} fusion(f32[]{:T(128)} %bitcast.17, s32[512]{0:T(512)S(1)} %get-tuple-element.63, f32[]{:T(128)} %bitcast.15, s32[512]{0:T(512)S(1)} %get-tuple-element.64, f32[]{:T(128)} %bitcast.13, s32[512]{0:T(512)S(1)} %get-tuple-element.65, f32[]{:T(128)} %bitcast.11, s32[512]{0:T(512)S(1)} %get-tuple-element.66, ...), kind=kOutput, calls=%fused_computation.30 | convolution fusion | flops 1651200000 | bytes 1337380 | tf_op jit(solution)/shard_map/dot_general | solution.py:53
  398.8 14.5 %fusion.17 = f32[2048,128]{1,0:T(8,128)S(1)} fusion(f32[]{:T(128)} %bitcast.17, f32[]{:T(128)} %bitcast.15, f32[]{:T(128)} %bitcast.13, f32[]{:T(128)} %bitcast.11, f32[]{:T(128)} %bitcast.9, f32[]{:T(128)} %bitcast.7, f32[]{:T(128)} %bitcast.5, f32[]{:T(128)} %bitcast.3, f32[]{:T(128)} %bitcast.1, s32[516]{0:T(1024)S(1)} %iota_multiply_fusion, ...), kind=kOutput, calls=%fused_computation.38 | convolution fusion | flops 1650803712 | bytes 1388596 | tf_op jit(solution)/shard_map/dot_general | solution.py:53
  416.9 39.1 %psum.91 = f32[]{:T(128)} all-reduce(f32[]{:T(128)} %get-tuple-element.57), channel_id=1, replica_groups=mesh['row'=16,'col'=8] {'row'}, use_global_device_ids=true, to_apply=%region_11.12 | all-reduce | flops 1 | bytes 8 | tf_op jit(solution)/shard_map/psum | solution.py:92
  460.4 34.2 %psum.92 = f32[]{:T(128)} all-reduce(f32[]{:T(128)} %get-tuple-element.12), channel_id=1, replica_groups=mesh['row'=16,'col'=8] {'row'}, use_global_device_ids=true, to_apply=%region_13.14 | all-reduce | flops 1 | bytes 8 | tf_op jit(solution)/shard_map/psum | solution.py:92
  504.1 14.1 %fusion.10 = f32[512,128]{1,0:T(8,128)S(1)} fusion(f32[]{:T(128)} %bitcast.17, s32[512]{0:T(512)S(1)} %get-tuple-element.63, f32[]{:T(128)} %bitcast.15, s32[512]{0:T(512)S(1)} %get-tuple-element.64, f32[]{:T(128)} %bitcast.13, s32[512]{0:T(512)S(1)} %get-tuple-element.65, f32[]{:T(128)} %bitcast.11, s32[512]{0:T(512)S(1)} %get-tuple-element.66, ...), kind=kOutput, calls=%fused_computation.29 | convolution fusion | flops 1651200000 | bytes 1337380 | tf_op jit(solution)/shard_map/dot_general | solution.py:53
  525.2 14.5 %fusion.16 = f32[2048,128]{1,0:T(8,128)S(1)} fusion(f32[]{:T(128)} %bitcast.17, f32[]{:T(128)} %bitcast.15, f32[]{:T(128)} %bitcast.13, f32[]{:T(128)} %bitcast.11, f32[]{:T(128)} %bitcast.9, f32[]{:T(128)} %bitcast.7, f32[]{:T(128)} %bitcast.5, f32[]{:T(128)} %bitcast.3, f32[]{:T(128)} %bitcast.1, s32[516]{0:T(1024)S(1)} %iota_multiply_fusion, ...), kind=kOutput, calls=%fused_computation.37 | convolution fusion | flops 1650803712 | bytes 1388596 | tf_op jit(solution)/shard_map/dot_general | solution.py:53
  543.3 39.1 %psum.93 = f32[]{:T(128)} all-reduce(f32[]{:T(128)} %get-tuple-element.59), channel_id=1, replica_groups=mesh['row'=16,'col'=8] {'row'}, use_global_device_ids=true, to_apply=%region_15.16 | all-reduce | flops 1 | bytes 8 | tf_op jit(solution)/shard_map/psum | solution.py:92
  587.0 33.8 %psum.94 = f32[]{:T(128)} all-reduce(f32[]{:T(128)} %get-tuple-element.10), channel_id=1, replica_groups=mesh['row'=16,'col'=8] {'row'}, use_global_device_ids=true, to_apply=%region_17.18 | all-reduce | flops 1 | bytes 8 | tf_op jit(solution)/shard_map/psum | solution.py:92
  630.5 14.1 %fusion.9 = f32[512,128]{1,0:T(8,128)S(1)} fusion(f32[]{:T(128)} %bitcast.17, s32[512]{0:T(512)S(1)} %get-tuple-element.63, f32[]{:T(128)} %bitcast.15, s32[512]{0:T(512)S(1)} %get-tuple-element.64, f32[]{:T(128)} %bitcast.13, s32[512]{0:T(512)S(1)} %get-tuple-element.65, f32[]{:T(128)} %bitcast.11, s32[512]{0:T(512)S(1)} %get-tuple-element.66, ...), kind=kOutput, calls=%fused_computation.28 | convolution fusion | flops 1651200000 | bytes 1337380 | tf_op jit(solution)/shard_map/dot_general | solution.py:53
  651.7 15.5 %fusion.15 = f32[2048,128]{1,0:T(8,128)S(1)} fusion(f32[]{:T(128)} %bitcast.17, f32[]{:T(128)} %bitcast.15, f32[]{:T(128)} %bitcast.13, f32[]{:T(128)} %bitcast.11, f32[]{:T(128)} %bitcast.9, f32[]{:T(128)} %bitcast.7, f32[]{:T(128)} %bitcast.5, f32[]{:T(128)} %bitcast.3, f32[]{:T(128)} %bitcast.1, s32[516]{0:T(1024)S(1)} %iota_multiply_fusion, ...), kind=kOutput, calls=%fused_computation.36 | convolution fusion | flops 1650803712 | bytes 1388596 | tf_op jit(solution)/shard_map/dot_general | solution.py:53
  670.7 39.1 %psum.95 = f32[]{:T(128)} all-reduce(f32[]{:T(128)} %get-tuple-element.61), channel_id=1, replica_groups=mesh['row'=16,'col'=8] {'row'}, use_global_device_ids=true, to_apply=%region_19.20 | all-reduce | flops 1 | bytes 8 | tf_op jit(solution)/shard_map/psum | solution.py:92
  (125 shorter events, 131.3 us)
Async XLA Ops:
  7.2 134.7 %all-reduce.4.cloned.1.call-start = ((), (), s32[]{:S(2)}) async-start(), calls=%async_computation.1 | async-start | bytes 2883584 | tf_op jit(solution)/shard_map/psum | solution.py:77
  33.2 19.3 %collective-permute-start = (bf16[8,128]{0,1:T(8,128)(2,1)S(1)}, bf16[8,128]{0,1:T(8,128)(2,1)S(1)}, u32[]{:S(2)}, u32[]{:S(2)}) collective-permute-start(bf16[8,128]{0,1:T(8,128)(2,1)S(1)} %get-tuple-element.36), channel_id=1, source_target_pairs={{0,1},{1,2},{2,3},{3,4},{4,5},{5,6},{6,7},{7,0},{8,9},{9,10},{10,1... | collective-permute-start | bytes 6152 | tf_op jit(solution)/shard_map/ppermute | solution.py:22
  34.7 17.8 %collective-permute-start.1 = (bf16[8,128]{0,1:T(8,128)(2,1)S(1)}, bf16[8,128]{0,1:T(8,128)(2,1)S(1)}, u32[]{:S(2)}, u32[]{:S(2)}) collective-permute-start(bf16[8,128]{0,1:T(8,128)(2,1)S(1)} %get-tuple-element.37), channel_id=1, source_target_pairs={{1,0},{2,1},{3,2},{4,3},{5,4},{6,5},{7,6},{0,7},{9,8},{10,9},{11,1... | collective-permute-start | bytes 6152 | tf_op jit(solution)/shard_map/ppermute | solution.py:24
  68.1 114.0 %all-gather.2.cloned.1.call-start = ((), (), s32[]{:S(2)}) async-start(), calls=%async_computation | async-start | bytes 1179648 | tf_op jit(solution)/shard_map/all_gather | solution.py:83
  182.8 6.9 collective-permute-start.5
  205.0 11.6 %collective-permute-start.6 = (f32[2,128]{1,0:T(2,128)S(1)}, f32[2,128]{1,0:T(2,128)S(1)}, u32[]{:S(2)}, u32[]{:S(2)}) collective-permute-start(f32[2,128]{1,0:T(2,128)S(1)} %get-tuple-element.34), channel_id=1, source_target_pairs={{0,8},{8,16},{16,24},{24,32},{32,40},{40,48},{48,56},{56,64},{64,7... | collective-permute-start | bytes 3080 | tf_op jit(solution)/shard_map/ppermute | solution.py:22
  205.1 11.5 %collective-permute-start.7 = (f32[2,128]{1,0:T(2,128)S(1)}, f32[2,128]{1,0:T(2,128)S(1)}, u32[]{:S(2)}, u32[]{:S(2)}) collective-permute-start(f32[2,128]{1,0:T(2,128)S(1)} %get-tuple-element.35), channel_id=1, source_target_pairs={{8,0},{16,8},{24,16},{32,24},{40,32},{48,40},{56,48},{64,56},{72,6... | collective-permute-start | bytes 3080 | tf_op jit(solution)/shard_map/ppermute | solution.py:24
  210.8 22.5 %collective-permute-start.2 = (f32[2,128]{0,1:T(8,128)S(1)}, f32[2,128]{0,1:T(8,128)S(1)}, u32[]{:S(2)}, u32[]{:S(2)}) collective-permute-start(f32[2,128]{0,1:T(8,128)S(1)} %get-tuple-element.32), channel_id=1, source_target_pairs={{0,8},{8,16},{16,24},{24,32},{32,40},{40,48},{48,56},{56,64},{64,7... | collective-permute-start | bytes 3080 | tf_op jit(solution)/shard_map/ppermute | solution.py:22
  210.9 22.5 %collective-permute-start.3 = (f32[2,128]{0,1:T(8,128)S(1)}, f32[2,128]{0,1:T(8,128)S(1)}, u32[]{:S(2)}, u32[]{:S(2)}) collective-permute-start(f32[2,128]{0,1:T(8,128)S(1)} %get-tuple-element.33), channel_id=1, source_target_pairs={{8,0},{16,8},{24,16},{32,24},{40,32},{48,40},{56,48},{64,56},{72,6... | collective-permute-start | bytes 3080 | tf_op jit(solution)/shard_map/ppermute | solution.py:24
  248.4 6.7 collective-permute-start.8
  248.4 6.9 collective-permute-start.9
  269.5 6.7 collective-permute-start.10
  269.6 7.1 collective-permute-start.11
  370.9 6.7 collective-permute-start.12
  371.0 6.7 collective-permute-start.13
  391.8 6.7 collective-permute-start.14
  391.9 6.9 collective-permute-start.15
  497.3 6.7 collective-permute-start.16
  518.2 6.7 collective-permute-start.18
  518.3 6.9 collective-permute-start.19
  623.5 6.9 collective-permute-start.20
  623.8 6.7 collective-permute-start.21
  644.7 6.7 collective-permute-start.22
  644.7 6.9 collective-permute-start.23
  (11 other events, 150.4 us)
Sparse Core Ops, SparseCore 0:
  68.2 73.6 all-reduce.3
  143.5 38.5 all-gather.1
where the time goes:
time: 728 us; the launch traced here: 722 us
  blocking collectives  284 us (39%)
  matrix products  199 us (27%)
  waiting for transfers between devices  113 us (16%)
  starting transfers between devices  66 us (9%)
  other arithmetic  30.2 us (4%)
  between operations  24.4 us (3%)
    psum x7, blocking collectives, inner_sum(): return lax.psum(jnp.sum(first_field * second_field), 'row')  258 us
    dot_general x12, matrix products, apply_band(): return jnp.dot(matrix, values.astype(jnp.float32), precision=FULL_PRECISION)  167 us
    ppermute x12, starting transfers between devices, extended(): lax.ppermute(head, axis, [((i + 1) % count, i) for i in range(count)])  63.5 us
    psum x1, waiting for transfers between devices, body(): column_gram, coarse_gram = lax.psum((column_part, coarse_part), 'col')  62 us
    all_gather x1, waiting for transfers between devices, body(): start_rows = lax.all_gather(row_start, 'col', axis=0, tiled=True)  39.1 us
    all_gather x1, blocking collectives, body(): columns = lax.all_gather(col_factor, 'row', axis=1, tiled=True)  25.9 us
  transfers between devices with their start and end apart: 26, of which 17 were waited for; matrix products, arithmetic and copies ran while one was open for 6% of the time, Pallas kernels for 0%

commit v1 on v0

--- a/solution.py
+++ b/solution.py
@@ -28,29 +28,34 @@
     return cells
 
 
-def down_matrix(weights, offsets, rows_out, rows_in):
-    outer = lax.broadcasted_iota(jnp.int32, (rows_out, rows_in), 0)
-    inner = lax.broadcasted_iota(jnp.int32, (rows_out, rows_in), 1)
-    total = jnp.zeros((rows_out, rows_in), jnp.float32)
+def tap_places(offsets):
+    reach = offsets + W
+    return reach // DEC, reach % DEC
+
+
+def blur_down(wide, weights, offsets, rows_out):
+    shifts, phases = tap_places(offsets)
+    quads = wide.reshape(wide.shape[0] // DEC, DEC, wide.shape[1])
+    total = jnp.zeros((rows_out, wide.shape[1]), jnp.float32)
     for number in range(weights.shape[0]):
-        target = DEC * outer + offsets[number] + W
-        total = total + jnp.where(inner == target, weights[number], jnp.float32(0.0))
+        piece = lax.dynamic_slice(
+            quads, (shifts[number], phases[number], 0), (rows_out, 1, wide.shape[1])
+        )[:, 0, :]
+        total = total + weights[number] * piece.astype(jnp.float32)
     return total
 
 
-def up_matrix(weights, offsets, rows_in, low_margin):
-    rows_out = (rows_in - 2 * low_margin) * DEC
-    outer = lax.broadcasted_iota(jnp.int32, (rows_out, rows_in), 0)
-    inner = lax.broadcasted_iota(jnp.int32, (rows_out, rows_in), 1)
-    total = jnp.zeros((rows_out, rows_in), jnp.float32)
+def blur_up(coarse_wide, weights, offsets, margin):
+    shifts, phases = tap_places(offsets)
+    rows = coarse_wide.shape[0] - 2 * margin
+    columns = coarse_wide.shape[1]
+    parts = [jnp.zeros((rows, columns), jnp.float32) for _ in range(DEC)]
     for number in range(weights.shape[0]):
-        target = outer + DEC * low_margin - offsets[number]
-        total = total + jnp.where(DEC * inner == target, weights[number], jnp.float32(0.0))
-    return total
-
-
-def apply_band(matrix, values):
-    return jnp.dot(matrix, values.astype(jnp.float32), precision=FULL_PRECISION)
+        piece = lax.dynamic_slice_in_dim(coarse_wide, margin + 2 - shifts[number], rows, 0)
+        for phase in range(DEC):
+            scale = jnp.where(phases[number] == phase, weights[number], jnp.float32(0.0))
+            parts[phase] = parts[phase] + scale * piece
+    return jnp.stack(parts, axis=1).reshape(rows * DEC, columns)
 
 
 def body(
@@ -59,8 +64,7 @@
     low_reach = (W + DEC - 1) // DEC
     columns = lax.all_gather(col_factor, "row", axis=1, tiled=True)
     column_wide = extended(columns, (("col", 0),), W)
-    column_down = down_matrix(blur_taps, offsets, columns.shape[0] // DEC, column_wide.shape[0])
-    coarse_columns = apply_band(column_down, column_wide)
+    coarse_columns = blur_down(column_wide, blur_taps, offsets, columns.shape[0] // DEC)
     merged = jnp.dot(response, band_factor, precision=FULL_PRECISION)
     multi_pairs = (merged[:, None, :] * columns.astype(jnp.float32)[None, :, :]).astype(
         jnp.bfloat16
@@ -82,31 +86,25 @@
     multi_sums, hyper_sums = lax.psum((multi_part, hyper_part), "col")
     start_rows = lax.all_gather(row_start, "col", axis=0, tiled=True)
 
-    def fine_rim(values, breadth):
-        return extended(values, (("row", 0),), breadth)
-
-    def coarse_rim(values):
-        return extended(values, (("row", 0),), low_reach)
-
     def inner_sum(first_field, second_field):
         return lax.psum(jnp.sum(first_field * second_field), "row")
 
     fine_rows = start_rows.shape[0]
     coarse_rows = fine_rows // DEC
-    lifting = up_matrix(blur_taps, offsets, coarse_rows + 2 * low_reach, low_reach)
-    lowering = down_matrix(blur_taps, offsets, coarse_rows, fine_rows + 2 * W)
+    fine_reach = W + DEC * low_reach
 
     def operate(values):
-        fine_wide = fine_rim(values, W)
-        coarse_wide = coarse_rim(apply_band(lowering, fine_wide))
-        restored = apply_band(lifting, coarse_wide)
+        fine_wide = extended(values, (("row", 0),), fine_reach)
+        coarse_wide = blur_down(fine_wide, blur_taps, offsets, coarse_rows + 2 * low_reach)
+        restored = blur_up(coarse_wide, blur_taps, offsets, low_reach)
         return (
             jnp.dot(restored, hyper_gram, precision=FULL_PRECISION)
             + jnp.dot(values, multi_gram, precision=FULL_PRECISION)
             + RIDGE_TERM * values
         )
 
-    right_side = apply_band(lifting, coarse_rim(hyper_sums)) + multi_sums
+    hyper_wide = extended(hyper_sums, (("row", 0),), low_reach)
+    right_side = blur_up(hyper_wide, blur_taps, offsets, low_reach) + multi_sums
     solution = start_rows
     residual = right_side - operate(solution)
     direction = residual

time: 728 us -> 648 us (0.89)
  matrix products: 199 us -> 34.2 us
  between operations: 24.4 us -> 125 us
  waiting for transfers between devices: 113 us -> 41.1 us
  local copies, waits for them, and re-layouts: 5.2 us -> 57.2 us
  starting transfers between devices: 66 us -> 37.8 us
  other arithmetic: 30.2 us -> 58.2 us
    dot_general x12 -> x0, matrix products: 167 us -> none  [apply_band(): return jnp.dot(matrix, values.astype(jnp.float32), precision=FULL_PRECISION)]
    psum x1, waiting for transfers between devices: 62 us -> 4.99 us  [body(): column_gram, coarse_gram = lax.psum((column_part, coarse_part), 'col')]
    ppermute x12 -> x7, starting transfers between devices: 63.5 us -> 35.9 us  [extended(): lax.ppermute(head, axis, [((i + 1) % count, i) for i in range(count)])]
    dynamic_slice x0 -> x6, local copies, waits for them, and re-layouts: none -> 26.8 us  [blur_down(): lax.dynamic_slice(quads, (shifts[number], phases[number], 0), (rows_out,...]
    add x11 -> x6, other arithmetic: 12.7 us -> 34.5 us  [blur_down(): total = total + weights[number] * piece.astype(jnp.float32)]
    concatenate x0 -> x10, local copies, waits for them, and re-layouts: none -> 14.9 us  [extended(): jnp.concatenate([lax.ppermute(tail, axis, [(i, (i + 1) % count) for i in...]
    all_gather x1, waiting for transfers between devices: 39.1 us -> 28.2 us  [body(): start_rows = lax.all_gather(row_start, 'col', axis=0, tiled=True)]
    another operation x0 -> x30, other arithmetic: none -> 9.72 us  [blur_up(): return jnp.stack(parts, axis=1).reshape(rows * DEC, columns)]
  transfers between devices with their start and end apart: 26 -> 16, of which waited for: 17 -> 10; matrix products, arithmetic and copies ran while one was open for 6% -> 3% of each run, Pallas kernels for 0% -> 0%
where the time goes in v1:
time: 648 us; the launch traced here: 637 us
  blocking collectives  284 us (44%)
  between operations  125 us (19%)
  other arithmetic  58.2 us (9%)
  local copies, waits for them, and re-layouts  57.2 us (9%)
  waiting for transfers between devices  41.1 us (6%)
  starting transfers between devices  37.8 us (6%)
  matrix products  34.2 us (5%)
    psum x7, blocking collectives, inner_sum(): return lax.psum(jnp.sum(first_field * second_field), 'row')  258 us
    ppermute x7, starting transfers between devices, extended(): lax.ppermute(head, axis, [((i + 1) % count, i) for i in range(count)])  35.9 us
    add x6, other arithmetic, blur_down(): total = total + weights[number] * piece.astype(jnp.float32)  34.5 us
    all_gather x1, waiting for transfers between devices, body(): start_rows = lax.all_gather(row_start, 'col', axis=0, tiled=True)  28.2 us
    dynamic_slice x6, local copies, waits for them, and re-layouts, blur_down(): lax.dynamic_slice(quads, (shifts[number], phases[number], 0), (rows_out,...  26.8 us
    all_gather x1, blocking collectives, body(): columns = lax.all_gather(col_factor, 'row', axis=1, tiled=True)  25.9 us
    concatenate x10, local copies, waits for them, and re-layouts, extended(): jnp.concatenate([lax.ppermute(tail, axis, [(i, (i + 1) % count) for i in...  14.9 us
  transfers between devices with their start and end apart: 16, of which 10 were waited for; matrix products, arithmetic and copies ran while one was open for 3% of the time, Pallas kernels for 0%

profile of v1, /device:TPU:0, one launch (start us, length us, event | category | flops | bytes accessed | tf_op | source)
XLA Modules:
  0.0 637.4 jit_solution(14981827791086670884)
XLA Ops:
  7.2 25.9 %all_gather.7 = bf16[512,128]{0,1:T(8,128)(2,1)S(1)} all-gather(bf16[512,8]{0,1:T(8,128)(2,1)} %param.11), channel_id=1, replica_groups=mesh['row'=16,'col'=8] {'row'}, dimensions={1}, use_global_device_ids=true | all-gather | bytes 139264 | tf_op jit(solution)/shard_map/all_gather | solution.py:65
  80.9 5.6 add_bitcast_fusion.4
  87.5 8.2 %fusion.10 = f32[512,128]{0,1:T(8,128)} fusion(bf16[96,512,128]{2,1,0:T(8,128)(2,1)} %param.9, f32[128,128]{0,1:T(8,128)S(1)} %copy.270, f32[96,128]{1,0:T(8,128)S(1)} %copy-done.7), kind=kOutput, calls=%fused_computation.17 | convolution fusion | flops 1613758464 | bytes 12959744 | tf_op jit(solution)/shard_map/kij,kjr->ir/dot_general | solution.py:76
  182.1 28.2 %all-gather.2.cloned.1.call-done = f32[2048,128]{0,1:T(8,128)} async-done(((f32[256,128]{0,1:T(8,128)}), f32[2048,128]{0,1:T(8,128)}) %all-gather.2.cloned.1.call-update) | async-done | bytes 1048592 | tf_op jit(solution)/shard_map/all_gather | solution.py:87
  211.9 5.5 collective-permute-start.5
  222.8 5.8 fusion.43
  233.5 5.6 collective-permute-start.7
  244.3 5.8 fusion.35
  255.3 39.2 %all-reduce = (f32[]{:T(128)}, f32[]{:T(128)}) all-reduce(f32[]{:T(128)} %get-tuple-element.11, f32[]{:T(128)} %get-tuple-element.10), channel_id=1, replica_groups=mesh['row'=16,'col'=8] {'row'}, use_global_device_ids=true, to_apply=%region_5.6 | all-reduce | flops 2 | bytes 16 | tf_op jit(solution)/shard_map/psum | solution.py:90
  296.6 33.8 %psum.90 = f32[]{:T(128)} all-reduce(f32[]{:T(128)} %multiply_reduce_fusion.5), channel_id=1, replica_groups=mesh['row'=16,'col'=8] {'row'}, use_global_device_ids=true, to_apply=%region_9.10 | all-reduce | flops 1 | bytes 8 | tf_op jit(solution)/shard_map/psum | solution.py:90
  332.1 5.6 collective-permute-start.9
  343.5 7.2 %constant_dynamic-slice_fusion.17 = (f32[516,1,128]{2,1,0:T(1,128)S(1)}, f32[516,1,128]{2,1,0:T(1,128)S(1)}, f32[516,1,128]{2,1,0:T(1,128)S(1)}, f32[516,1,128]{...) fusion(f32[520,4,128]{2,1,0:T(4,128)} %bitcast.340, ...), kind=kLoop, calls=%fused_computation.222 | loop fusion | bytes 4755528 | tf_op jit(solution)/shard_map/dynamic_slice | solution.py:41
  350.7 5.8 fusion.27
  362.6 39.2 %psum.91 = f32[]{:T(128)} all-reduce(f32[]{:T(128)} %get-tuple-element.120), channel_id=1, replica_groups=mesh['row'=16,'col'=8] {'row'}, use_global_device_ids=true, to_apply=%region_11.12 | all-reduce | flops 1 | bytes 8 | tf_op jit(solution)/shard_map/psum | solution.py:90
  406.1 33.8 %psum.92 = f32[]{:T(128)} all-reduce(f32[]{:T(128)} %get-tuple-element.20), channel_id=1, replica_groups=mesh['row'=16,'col'=8] {'row'}, use_global_device_ids=true, to_apply=%region_13.14 | all-reduce | flops 1 | bytes 8 | tf_op jit(solution)/shard_map/psum | solution.py:90
  442.7 5.8 collective-permute-start.11
  454.4 7.2 %constant_dynamic-slice_fusion.8 = (f32[516,1,128]{2,1,0:T(1,128)S(1)}, f32[516,1,128]{2,1,0:T(1,128)S(1)}, f32[516,1,128]{2,1,0:T(1,128)S(1)}, f32[516,1,128]{2...) fusion(f32[520,4,128]{2,1,0:T(4,128)} %bitcast.341, ...), kind=kLoop, calls=%fused_computation.213 | loop fusion | bytes 4755528 | tf_op jit(solution)/shard_map/dynamic_slice | solution.py:41
  461.6 5.8 fusion.19
  473.4 39.2 %psum.93 = f32[]{:T(128)} all-reduce(f32[]{:T(128)} %get-tuple-element.122), channel_id=1, replica_groups=mesh['row'=16,'col'=8] {'row'}, use_global_device_ids=true, to_apply=%region_15.16 | all-reduce | flops 1 | bytes 8 | tf_op jit(solution)/shard_map/psum | solution.py:90
  517.3 33.8 %psum.94 = f32[]{:T(128)} all-reduce(f32[]{:T(128)} %get-tuple-element.18), channel_id=1, replica_groups=mesh['row'=16,'col'=8] {'row'}, use_global_device_ids=true, to_apply=%region_17.18 | all-reduce | flops 1 | bytes 8 | tf_op jit(solution)/shard_map/psum | solution.py:90
  555.6 5.5 collective-permute-start.13
  568.0 7.2 %constant_dynamic-slice_fusion.44 = (f32[516,1,128]{2,1,0:T(1,128)S(1)}, f32[516,1,128]{2,1,0:T(1,128)S(1)}, f32[516,1,128]{2,1,0:T(1,128)S(1)}, f32[516,1,128]{...) fusion(f32[520,4,128]{2,1,0:T(4,128)} %bitcast.337, ...), kind=kLoop, calls=%fused_computation.249 | loop fusion | bytes 4755528 | tf_op jit(solution)/shard_map/dynamic_slice | solution.py:41
  575.3 5.8 fusion.11
  587.2 39.1 %psum.95 = f32[]{:T(128)} all-reduce(f32[]{:T(128)} %get-tuple-element.124), channel_id=1, replica_groups=mesh['row'=16,'col'=8] {'row'}, use_global_device_ids=true, to_apply=%region_19.20 | all-reduce | flops 1 | bytes 8 | tf_op jit(solution)/shard_map/psum | solution.py:90
  (141 shorter events, 108.0 us)
Async XLA Ops:
  7.2 49.5 %copy-start = (f32[2,96]{1,0:T(2,128)S(1)}, f32[2,96]{1,0:T(2,128)}, u32[]{:S(2)}) copy-start(f32[2,96]{1,0:T(2,128)} %param.13) | copy-start | bytes 2308
  7.2 48.8 %copy-start.9 = (f32[9]{0:T(128)S(1)}, f32[9]{0:T(128)}, u32[]{:S(2)}) copy-start(f32[9]{0:T(128)} %param.14) | copy-start | bytes 112
  7.2 49.5 %copy-start.7 = (f32[96,128]{1,0:T(8,128)S(1)}, f32[96,128]{1,0:T(8,128)}, u32[]{:S(2)}) copy-start(f32[96,128]{1,0:T(8,128)} %param.12) | copy-start | bytes 147460
  7.2 162.3 %all-reduce.4.cloned.1.call-start = ((), (), s32[]{:S(2)}) async-start(), calls=%async_computation.1 | async-start | bytes 2883584 | tf_op jit(solution)/shard_map/psum | solution.py:81
  33.3 46.9 %collective-permute-start = (bf16[8,128]{1,0:T(8,128)(2,1)S(1)}, bf16[8,128]{1,0:T(8,128)(2,1)S(1)}, u32[]{:S(2)}, u32[]{:S(2)}) collective-permute-start(bf16[8,128]{1,0:T(8,128)(2,1)S(1)} %get-tuple-element.90), channel_id=1, source_target_pairs={{0,1},{1,2},{2,3},{3,4},{4,5},{5,6},{6,7},{7,0},{8,9},{9,10},{10,1... | collective-permute-start | bytes 6152 | tf_op jit(solution)/shard_map/ppermute | solution.py:22
  34.9 45.3 %collective-permute-start.1 = (bf16[8,128]{1,0:T(8,128)(2,1)S(1)}, bf16[8,128]{1,0:T(8,128)(2,1)S(1)}, u32[]{:S(2)}, u32[]{:S(2)}) collective-permute-start(bf16[8,128]{1,0:T(8,128)(2,1)S(1)} %get-tuple-element.91), channel_id=1, source_target_pairs={{1,0},{2,1},{3,2},{4,3},{5,4},{6,5},{7,6},{0,7},{9,8},{10,9},{11,1... | collective-permute-start | bytes 6152 | tf_op jit(solution)/shard_map/ppermute | solution.py:24
  95.7 114.6 %all-gather.2.cloned.1.call-start = ((), (), s32[]{:S(2)}) async-start(), calls=%async_computation | async-start | bytes 1179648 | tf_op jit(solution)/shard_map/all_gather | solution.py:87
  170.5 7.7 %collective-permute-start.2 = (f32[2,128]{0,1:T(8,128)S(1)}, f32[2,128]{0,1:T(8,128)S(1)}, u32[]{:S(2)}, u32[]{:S(2)}) collective-permute-start(f32[2,128]{0,1:T(8,128)S(1)} %get-tuple-element.79), channel_id=1, source_target_pairs={{0,8},{8,16},{16,24},{24,32},{32,40},{40,48},{48,56},{56,64},{64,7... | collective-permute-start | bytes 3080 | tf_op jit(solution)/shard_map/ppermute | solution.py:22
  170.5 7.6 %collective-permute-start.3 = (f32[2,128]{0,1:T(8,128)S(1)}, f32[2,128]{0,1:T(8,128)S(1)}, u32[]{:S(2)}, u32[]{:S(2)}) collective-permute-start(f32[2,128]{0,1:T(8,128)S(1)} %get-tuple-element.80), channel_id=1, source_target_pairs={{8,0},{16,8},{24,16},{32,24},{40,32},{48,40},{56,48},{64,56},{72,6... | collective-permute-start | bytes 3080 | tf_op jit(solution)/shard_map/ppermute | solution.py:24
  211.9 7.5 %collective-permute-start.4 = (f32[16,128]{0,1:T(8,128)}, f32[16,128]{0,1:T(8,128)S(1)}, u32[]{:S(2)}, u32[]{:S(2)}) collective-permute-start(f32[16,128]{0,1:T(8,128)} %get-tuple-element.78), channel_id=1, source_target_pairs={{0,8},{8,16},{16,24},{24,32},{32,40},{40,48},{48,56},{56,64},{64,7... | collective-permute-start | bytes 24584 | tf_op jit(solution)/shard_map/ppermute | solution.py:22
  211.9 7.5 %collective-permute-start.5 = (f32[16,128]{0,1:T(8,128)S(1)}, f32[16,128]{0,1:T(8,128)S(1)}, u32[]{:S(2)}, u32[]{:S(2)}) collective-permute-start(f32[16,128]{0,1:T(8,128)S(1)} %get-tuple-element.77), channel_id=1, source_target_pairs={{8,0},{16,8},{24,16},{32,24},{40,32},{48,40},{56,48},{64,56},{72,6... | collective-permute-start | bytes 24584 | tf_op jit(solution)/shard_map/ppermute | solution.py:24
  217.9 1.6 copy-start.4
  230.6 1.2 copy-start.5
  230.6 1.5 copy-start.6
  233.5 7.3 %collective-permute-start.6 = (f32[16,128]{0,1:T(8,128)S(1)}, f32[16,128]{0,1:T(8,128)S(1)}, u32[]{:S(2)}, u32[]{:S(2)}) collective-permute-start(f32[16,128]{0,1:T(8,128)S(1)} %get-tuple-element.76), channel_id=1, source_target_pairs={{0,8},{8,16},{16,24},{24,32},{32,40},{40,48},{48,56},{56,64},{64,7... | collective-permute-start | bytes 24584 | tf_op jit(solution)/shard_map/ppermute | solution.py:22
  233.5 7.5 %collective-permute-start.7 = (f32[16,128]{0,1:T(8,128)S(1)}, f32[16,128]{0,1:T(8,128)S(1)}, u32[]{:S(2)}, u32[]{:S(2)}) collective-permute-start(f32[16,128]{0,1:T(8,128)S(1)} %get-tuple-element.75), channel_id=1, source_target_pairs={{8,0},{16,8},{24,16},{32,24},{40,32},{48,40},{56,48},{64,56},{72,6... | collective-permute-start | bytes 24584 | tf_op jit(solution)/shard_map/ppermute | solution.py:24
  332.0 7.3 %collective-permute-start.8 = (f32[16,128]{0,1:T(8,128)S(1)}, f32[16,128]{0,1:T(8,128)S(1)}, u32[]{:S(2)}, u32[]{:S(2)}) collective-permute-start(f32[16,128]{0,1:T(8,128)S(1)} %get-tuple-element.74), channel_id=1, source_target_pairs={{0,8},{8,16},{16,24},{24,32},{32,40},{40,48},{48,56},{56,64},{64,7... | collective-permute-start | bytes 24584 | tf_op jit(solution)/shard_map/ppermute | solution.py:22
  332.1 7.5 %collective-permute-start.9 = (f32[16,128]{0,1:T(8,128)S(1)}, f32[16,128]{0,1:T(8,128)S(1)}, u32[]{:S(2)}, u32[]{:S(2)}) collective-permute-start(f32[16,128]{0,1:T(8,128)S(1)} %get-tuple-element.73), channel_id=1, source_target_pairs={{8,0},{16,8},{24,16},{32,24},{40,32},{48,40},{56,48},{64,56},{72,6... | collective-permute-start | bytes 24584 | tf_op jit(solution)/shard_map/ppermute | solution.py:24
  442.7 7.3 %collective-permute-start.10 = (f32[16,128]{0,1:T(8,128)S(1)}, f32[16,128]{0,1:T(8,128)S(1)}, u32[]{:S(2)}, u32[]{:S(2)}) collective-permute-start(f32[16,128]{0,1:T(8,128)S(1)} %get-tuple-element.72), channel_id=1, source_target_pairs={{0,8},{8,16},{16,24},{24,32},{32,40},{40,48},{48,56},{56,64},{64,7... | collective-permute-start | bytes 24584 | tf_op jit(solution)/shard_map/ppermute | solution.py:22
  442.7 7.7 %collective-permute-start.11 = (f32[16,128]{0,1:T(8,128)S(1)}, f32[16,128]{0,1:T(8,128)S(1)}, u32[]{:S(2)}, u32[]{:S(2)}) collective-permute-start(f32[16,128]{0,1:T(8,128)S(1)} %get-tuple-element.71), channel_id=1, source_target_pairs={{8,0},{16,8},{24,16},{32,24},{40,32},{48,40},{56,48},{64,56},{72,6... | collective-permute-start | bytes 24584 | tf_op jit(solution)/shard_map/ppermute | solution.py:24
  555.6 7.5 %collective-permute-start.12 = (f32[16,128]{0,1:T(8,128)}, f32[16,128]{0,1:T(8,128)S(1)}, u32[]{:S(2)}, u32[]{:S(2)}) collective-permute-start(f32[16,128]{0,1:T(8,128)} %get-tuple-element.70), channel_id=1, source_target_pairs={{0,8},{8,16},{16,24},{24,32},{32,40},{40,48},{48,56},{56,64},{64,7... | collective-permute-start | bytes 24584 | tf_op jit(solution)/shard_map/ppermute | solution.py:22
  555.6 7.5 %collective-permute-start.13 = (f32[16,128]{0,1:T(8,128)S(1)}, f32[16,128]{0,1:T(8,128)S(1)}, u32[]{:S(2)}, u32[]{:S(2)}) collective-permute-start(f32[16,128]{0,1:T(8,128)S(1)} %get-tuple-element.69), channel_id=1, source_target_pairs={{8,0},{16,8},{24,16},{32,24},{40,32},{48,40},{56,48},{64,56},{72,6... | collective-permute-start | bytes 24584 | tf_op jit(solution)/shard_map/ppermute | solution.py:24
  583.2 1.2 copy-start.3
  584.4 46.0 %copy-start.1 = (f32[2,96]{1,0:T(2,128)S(1)}, f32[2,96]{1,0:T(2,128)}, u32[]{:S(2)}) copy-start(f32[2,96]{1,0:T(2,128)} %param.13) | copy-start | bytes 2308
  (2 other events, 1.9 us)
Sparse Core Ops, SparseCore 0:
  95.8 73.6 all-reduce.3
  171.7 38.5 all-gather.1
